TPU v7x, 256 devices: a whole 4x4x8 slice. The times are simulated.
256 devices in a mesh: rep: 16 (over x, z_lo, core), tp: 16 (over z_hi, y).
Axes of the slice: x: 4, y: 4, z: 8 (z_hi: 4, z_lo: 2; z = z_hi * 2 + z_lo), core: 2. Of those that a mesh axis runs over, the one named last changes fastest.
Arguments:
- activations: bfloat16 [16, 256, 2560], P('rep', 'tp'), may hold values from -6 to 6
- out_grad: bfloat16 [16, 256, 2560], P('rep', 'tp'), may hold values from -6 to 6
- gate_weight: bfloat16 [16, 2560, 6912], P('rep', None, 'tp'), may hold values from -6 to 6
- up_weight: bfloat16 [16, 2560, 6912], P('rep', None, 'tp'), may hold values from -6 to 6
- down_weight: bfloat16 [16, 6912, 2560], P('rep', 'tp'), may hold values from -6 to 6
- step_index: int32 [1], replicated, may hold values from 0 to 999
Outputs:
- layer_out: bfloat16 [16, 256, 2560], P('rep', 'tp')
- grad_in: bfloat16 [16, 256, 2560], P('rep', 'tp')
- new_gate: bfloat16 [16, 2560, 6912], P('rep', None, 'tp')
- new_up: bfloat16 [16, 2560, 6912], P('rep', None, 'tp')
- new_down: bfloat16 [16, 6912, 2560], P('rep', 'tp')
All inputs are finite; a program needn't handle non-finite values.
Results may differ from a plain program's by a relative error of at most 0.0052.
Values may be sent and summed in bfloat16 or wider, within the bound.
A program may use at most 128 MiB of HBM per device.

v0:
```python
from functools import partial
import math
import jax
import jax.numpy as jnp
from jax import lax
from jax.sharding import PartitionSpec as P

D = 2560
FF = 6912
learn_rate = 0.8


def for_sending(x):

    def short(part):
        return part.astype(jnp.bfloat16) if part.dtype == jnp.float32 else part

    return jax.tree.map(short, x)


def shifted(x, axis, by):
    devices = lax.axis_size(axis)
    return lax.ppermute(x, axis, [(i, (i + by) % devices) for i in range(devices)])


def partner_copy(stepped, distance, loop_size):
    return shifted(
        (for_sending(stepped[0]), for_sending(stepped[1]), for_sending(stepped[2])), "rep", distance
    )


def shards(activations, out_grad, gate_weight, up_weight, down_weight, step_index):
    tokens_local = activations[0]
    grads_local = out_grad[0]
    gate_w = gate_weight[0]
    up_w = up_weight[0]
    down_w = down_weight[0]
    width_scale = 1.0 / math.sqrt(D)
    hidden_scale = 1.0 / math.sqrt(FF)
    gathered = lax.all_gather(tokens_local, "tp", axis=0, tiled=True)
    gate_pre = jnp.dot(gathered, gate_w, preferred_element_type=jnp.float32) * width_scale
    up_pre = jnp.dot(gathered, up_w, preferred_element_type=jnp.float32) * width_scale
    sigmoid_gate = jax.nn.sigmoid(gate_pre)
    activated = gate_pre * sigmoid_gate
    hidden = (activated * up_pre).astype(jnp.bfloat16)
    rows_hidden = hidden
    layer_part = lax.psum_scatter(
        jnp.dot(rows_hidden, down_w, preferred_element_type=jnp.float32) * hidden_scale,
        "tp",
        scatter_dimension=0,
        tiled=True,
    )
    piece = lax.all_gather(grads_local, "tp", axis=0, tiled=True)
    rows_hidden = hidden
    down_sum = jnp.einsum("tf,td->fd", rows_hidden, piece, preferred_element_type=jnp.float32)
    back_rows = jnp.einsum("td,fd->tf", piece, down_w, preferred_element_type=jnp.float32)
    down_sum, back_hidden = (down_sum, back_rows)
    grad_down = down_sum * hidden_scale
    d_hidden = back_hidden * hidden_scale
    d_gate = (d_hidden * up_pre * (sigmoid_gate * (1.0 + gate_pre * (1.0 - sigmoid_gate)))).astype(
        jnp.bfloat16
    )
    d_up = (d_hidden * activated).astype(jnp.bfloat16)
    grad_gate = (
        jnp.einsum("td,tf->df", gathered, d_gate, preferred_element_type=jnp.float32) * width_scale
    )
    grad_upw = (
        jnp.einsum("td,tf->df", gathered, d_up, preferred_element_type=jnp.float32) * width_scale
    )
    grad_part = lax.psum_scatter(
        (
            jnp.einsum("tf,df->td", d_gate, gate_w, preferred_element_type=jnp.float32)
            + jnp.einsum("tf,df->td", d_up, up_w, preferred_element_type=jnp.float32)
        )
        * width_scale,
        "tp",
        scatter_dimension=0,
        tiled=True,
    )
    stepped = (
        (gate_w.astype(jnp.float32) - learn_rate * grad_gate).astype(jnp.bfloat16),
        (up_w.astype(jnp.float32) - learn_rate * grad_upw).astype(jnp.bfloat16),
        (down_w.astype(jnp.float32) - learn_rate * grad_down).astype(jnp.bfloat16),
    )
    loop_size = lax.axis_size("rep")
    levels = loop_size.bit_length() - 1
    branches = [
        partial(partner_copy, distance=1 << level, loop_size=loop_size) for level in range(levels)
    ]
    chosen = step_index[0] % levels
    received = lax.switch(chosen, branches, stepped)
    averaged = tuple(
        (
            ((mine.astype(jnp.float32) + theirs.astype(jnp.float32)) * 0.5).astype(jnp.bfloat16)
            for mine, theirs in zip(stepped, received)
        )
    )
    return (
        layer_part.astype(jnp.bfloat16)[None],
        grad_part.astype(jnp.bfloat16)[None],
        averaged[0][None],
        averaged[1][None],
        averaged[2][None],
    )


def solution(mesh):
    in_specs = (
        P("rep", "tp", None),
        P("rep", "tp", None),
        P("rep", None, "tp"),
        P("rep", None, "tp"),
        P("rep", "tp", None),
        P(),
    )
    out_specs = (
        P("rep", "tp", None),
        P("rep", "tp", None),
        P("rep", None, "tp"),
        P("rep", None, "tp"),
        P("rep", "tp", None),
    )
    return jax.shard_map(shards, mesh=mesh, in_specs=in_specs, out_specs=out_specs, check_vma=False)
```

profile of v0, /device:TPU:6, one launch (start us, length us, event | category | flops | bytes accessed | tf_op | source)
XLA Modules:
  0.0 318.3 jit_solution(7605034518232308111)
XLA Ops:
  7.2 0.0 all-gather.5.cloned.1.call-start
  7.2 0.7 all-gather.5.cloned.1.call-update
  7.9 0.0 all-gather.7.cloned.1.call-start
  7.9 0.7 all-gather.7.cloned.1.call-update
  8.7 0.0 reduce-scatter.5.cloned.1.call-start
  8.7 59.0 %all-gather.5.cloned.1.call-done = bf16[1,256,2560]{2,1,0:T(8,128)(2,1)} async-done(((bf16[1,16,2560]{2,1,0:T(8,128)(2,1)}), bf16[1,256,2560]{2,1,0:T(8,128)(2,1)}) %all-gather.5.cloned.1.call-update) | async-done | bytes 1310736 | tf_op jit(solution)/shard_map/all_gather | solution.py:40
  67.7 0.0 copy-start.3
  67.7 0.0 copy-start.7
  67.7 3.7 %fusion.39 = f32[256,432]{0,1:T(8,128)} fusion(bf16[1,2560,432]{1,2,0:T(8,128)(2,1)} %param.13, bf16[1,256,2560]{2,1,0:T(8,128)(2,1)} %all-gather.5.cloned.1.call-done), kind=kOutput, calls=%fused_computation.43 | convolution fusion | flops 566341632 | bytes 3964928 | tf_op jit(solution)/shard_map/dot_general | solution.py:42
  71.4 0.0 copy-done.3
  71.4 0.0 copy-done.7
  71.4 0.0 copy-start
  71.4 1.5 fusion.34
  72.9 48.9 %all-gather.7.cloned.1.call-done = bf16[1,256,2560]{2,1,0:T(8,128)(2,1)} async-done(((bf16[1,16,2560]{2,1,0:T(8,128)(2,1)}), bf16[1,256,2560]{2,1,0:T(8,128)(2,1)}) %all-gather.7.cloned.1.call-update) | async-done | bytes 1310736 | tf_op jit(solution)/shard_map/all_gather | solution.py:53
  121.8 0.0 copy-done
  121.8 0.0 copy-start.4
  121.8 3.2 %multiply_convert_fusion = (bf16[256,432]{0,1:T(8,128)(2,1)S(1)}, bf16[256,432]{0,1:T(8,128)(2,1)S(1)}, bf16[256,432]{0,1:T(8,128)(2,1)}) fusion(f32[256,432]{0,1:T(8,128)} %fusion.34, f32[256,432]{0,1:T(8,128)} %fusion.39, bf16[1,432,2560]{2,1,0:T(8,128)(2,1)S(1)} %copy-done, bf16[1,256,2560]{2,1,0:T(8,128)(2,1)} %all-gather.7.cloned.1.call-done), kind=kOutput, calls=%fused_computation.45 | convolution fusion | flops 568000512 | bytes 5070848 | tf_op jit(solution)/shard_map/td,fd->tf/dot_general | solution.py:56
  125.0 0.0 copy-start.8
  125.0 0.0 copy-start.10
  125.1 0.0 copy-done.4
  125.1 0.0 copy-start.1
  125.1 0.9 fusion.24
  125.9 0.0 copy-done.8
  125.9 0.0 copy-done.10
  125.9 0.9 copy-done.1
  126.8 2.4 fusion.14
  129.3 0.0 reduce-scatter.5.cloned.1.call-update
  129.3 0.0 reduce-scatter.3.cloned.1.call-start
  129.3 3.3 %convolution_multiply_fusion.3 = f32[256,2560]{1,0:T(8,128)} fusion(bf16[256,432]{0,1:T(8,128)(2,1)} %get-tuple-element.88, bf16[1,432,2560]{2,1,0:T(8,128)(2,1)S(1)} %copy-done), kind=kOutput, calls=%fused_computation.22 | convolution fusion | flops 566886400 | bytes 5054464 | tf_op jit(solution)/shard_map/dot_general | solution.py:48
  132.6 0.0 reduce-scatter.3.cloned.1.call-update
  133.3 0.0 copy-start.2
  133.3 0.0 copy-start.11
  133.3 2.3 fusion.13
  135.7 0.0 copy-done.2
  135.7 0.0 copy-done.11
  135.7 0.0 copy-start.6
  135.7 0.0 copy-start.5
  135.7 0.0 copy-start.9
  135.7 0.8 fusion.11
  136.5 1.6 copy-done.5
  138.1 0.0 copy-done.9
  138.1 2.1 fusion.12
  140.2 0.0 copy-done.6
  140.2 145.0 %conditional.4 = (bf16[2560,432]{0,1:T(8,128)(2,1)}, bf16[2560,432]{0,1:T(8,128)(2,1)}, bf16[432,2560]{1,0:T(8,128)(2,1)}) conditional(s32[]{:T(128)} %clamp.3, (bf16[2560,432]{0,1:T(8,128)(2,1)}, bf16[2560,432]{0,1:T(8,128)(2,1)S(1)}, bf16[432,2560]{1,0:T(8,128)(2,1)S(1)}) %tuple.58, (bf16[2560,432]{0,1:T(8,128)(2,1)}, ...), branch_computations={%region_2.3_spmd, %region_3.4_spmd, %region_4.5_spmd, %region_5.6_... | conditional | bytes 26542224
  140.2 1.5 collective-permute-start.9
  141.7 2.1 collective-permute-start.10
  143.8 1.5 collective-permute-start.11
  145.2 47.8 %collective-permute-done.9 = bf16[2560,432]{0,1:T(8,128)(2,1)} collective-permute-done((bf16[2560,432]{0,1:T(8,128)(2,1)}, bf16[2560,432]{0,1:T(8,128)(2,1)}, u32[]{:S(2)}, u32[]{:S(2)}) %collective-permute-start.9) | collective-permute-done | bytes 2211872 | tf_op jit(solution)/shard_map/cond/branch_3_fun/ppermute | solution.py:23
  193.0 47.4 %collective-permute-done.10 = bf16[2560,432]{0,1:T(8,128)(2,1)} collective-permute-done((bf16[2560,432]{0,1:T(8,128)(2,1)S(1)}, bf16[2560,432]{0,1:T(8,128)(2,1)}, u32[]{:S(2)}, u32[]{:S(2)}) %collective-permute-start.10) | collective-permute-done | bytes 2211872 | tf_op jit(solution)/shard_map/cond/branch_3_fun/ppermute | solution.py:23
  240.4 44.8 %collective-permute-done.11 = bf16[432,2560]{1,0:T(8,128)(2,1)} collective-permute-done((bf16[432,2560]{1,0:T(8,128)(2,1)S(1)}, bf16[432,2560]{1,0:T(8,128)(2,1)}, u32[]{:S(2)}, u32[]{:S(2)}) %collective-permute-start.11) | collective-permute-done | bytes 2211872 | tf_op jit(solution)/shard_map/cond/branch_3_fun/ppermute | solution.py:23
  285.3 4.3 %fusion.17 = bf16[1,432,2560]{2,1,0:T(8,128)(2,1)} fusion(bf16[432,2560]{1,0:T(8,128)(2,1)} %get-tuple-element.85, bf16[432,2560]{1,0:T(8,128)(2,1)} %copy-done.6), kind=kLoop, calls=%fused_computation.25 | loop fusion | flops 5529600 | bytes 6635520 | tf_op jit(solution)/shard_map/broadcast_in_dim | solution.py:103
  289.5 6.4 %fusion.15 = (bf16[1,2560,432]{1,2,0:T(8,128)(2,1)}, bf16[1,2560,432]{1,2,0:T(8,128)(2,1)}) fusion(bf16[2560,432]{0,1:T(8,128)(2,1)} %get-tuple-element.83, bf16[2560,432]{0,1:T(8,128)(2,1)} %fusion.12, bf16[2560,432]{0,1:T(8,128)(2,1)} %get-tuple-element.84, bf16[2560,432]{0,1:T(8,128)(2,1)S(1)} %fusion.11), kind=kLoop, calls=%fused_computation.23 | loop fusion | flops 11059200 | bytes 13271040 | tf_op jit(solution)/shard_map/broadcast_in_dim | solution.py:101
  295.9 0.0 reduce-scatter.5.cloned.1.call-done
  295.9 1.6 convert_bitcast_fusion
  297.5 12.7 %reduce-scatter.3.cloned.1.call-done = f32[16,2560]{1,0:T(8,128)} async-done(((f32[256,2560]{1,0:T(8,128)}), f32[16,2560]{1,0:T(8,128)}) %reduce-scatter.3.cloned.1.call-update) | async-done | bytes 163856 | tf_op jit(solution)/shard_map/reduce_scatter | solution.py:47
  310.2 1.6 convert_bitcast_fusion.1
Async XLA Ops:
  7.2 60.5 %all-gather.5.cloned.1.call-start = ((), (), s32[]{:S(2)}) async-start(), calls=%async_computation.4 | async-start | bytes 1392640 | tf_op jit(solution)/shard_map/all_gather | solution.py:40
  7.9 113.9 %all-gather.7.cloned.1.call-start = ((), (), s32[]{:S(2)}) async-start(), calls=%async_computation.5 | async-start | bytes 1392640 | tf_op jit(solution)/shard_map/all_gather | solution.py:53
  8.7 287.3 %reduce-scatter.5.cloned.1.call-start = ((), (), s32[]{:S(2)}) async-start(), calls=%async_computation.3 | async-start | bytes 2785280 | tf_op jit(solution)/shard_map/reduce_scatter | solution.py:70
  67.7 3.7 %copy-start.3 = (bf16[1,2560,432]{1,2,0:T(8,128)(2,1)S(1)}, bf16[1,2560,432]{1,2,0:T(8,128)(2,1)}, u32[]{:S(2)}) copy-start(bf16[1,2560,432]{1,2,0:T(8,128)(2,1)} %param.12) | copy-start | bytes 6635524
  67.7 3.7 %copy-start.7 = (bf16[1,256,2560]{2,1,0:T(8,128)(2,1)S(1)}, bf16[1,256,2560]{2,1,0:T(8,128)(2,1)}, u32[]{:S(2)}) copy-start(bf16[1,256,2560]{2,1,0:T(8,128)(2,1)} %all-gather.5.cloned.1.call-done) | copy-start | bytes 3932164
  71.4 50.5 %copy-start = (bf16[1,432,2560]{2,1,0:T(8,128)(2,1)S(1)}, bf16[1,432,2560]{2,1,0:T(8,128)(2,1)}, u32[]{:S(2)}) copy-start(bf16[1,432,2560]{2,1,0:T(8,128)(2,1)} %param.14) | copy-start | bytes 6635524
  121.8 3.2 %copy-start.4 = (bf16[1,2560,432]{1,2,0:T(8,128)(2,1)S(1)}, bf16[1,2560,432]{1,2,0:T(8,128)(2,1)}, u32[]{:S(2)}) copy-start(bf16[1,2560,432]{1,2,0:T(8,128)(2,1)} %param.12) | copy-start | bytes 6635524
  125.0 0.9 copy-start.8
  125.0 0.9 copy-start.10
  125.1 1.8 copy-start.1
  129.3 180.9 %reduce-scatter.3.cloned.1.call-start = ((), (), s32[]{:S(2)}) async-start(), calls=%async_computation.2 | async-start | bytes 2785280 | tf_op jit(solution)/shard_map/reduce_scatter | solution.py:47
  133.3 2.4 copy-start.2
  133.3 2.3 copy-start.11
  135.7 4.5 %copy-start.6 = (bf16[432,2560]{1,0:T(8,128)(2,1)}, bf16[432,2560]{1,0:T(8,128)(2,1)S(1)}, u32[]{:S(2)}) copy-start(bf16[432,2560]{1,0:T(8,128)(2,1)S(1)} %fusion.13) | copy-start | bytes 6635524
  135.7 2.4 copy-start.5
  135.7 2.4 copy-start.9
  140.2 52.8 %collective-permute-start.9 = (bf16[2560,432]{0,1:T(8,128)(2,1)}, bf16[2560,432]{0,1:T(8,128)(2,1)}, u32[]{:S(2)}, u32[]{:S(2)}) collective-permute-start(bf16[2560,432]{0,1:T(8,128)(2,1)} %get-tuple-element.51), channel_id=1, source_target_pairs={{0,128},{16,144},{32,160},{48,176},{64,192},{80,208},{96,224},{112... | collective-permute-start | bytes 6635528 | tf_op jit(solution)/shard_map/cond/branch_3_fun/ppermute | solution.py:23
  141.7 98.7 %collective-permute-start.10 = (bf16[2560,432]{0,1:T(8,128)(2,1)S(1)}, bf16[2560,432]{0,1:T(8,128)(2,1)}, u32[]{:S(2)}, u32[]{:S(2)}) collective-permute-start(bf16[2560,432]{0,1:T(8,128)(2,1)S(1)} %get-tuple-element.52), channel_id=1, source_target_pairs={{0,128},{16,144},{32,160},{48,176},{64,192},{80,208},{96,224},{112... | collective-permute-start | bytes 6635528 | tf_op jit(solution)/shard_map/cond/branch_3_fun/ppermute | solution.py:23
  143.8 141.5 %collective-permute-start.11 = (bf16[432,2560]{1,0:T(8,128)(2,1)S(1)}, bf16[432,2560]{1,0:T(8,128)(2,1)}, u32[]{:S(2)}, u32[]{:S(2)}) collective-permute-start(bf16[432,2560]{1,0:T(8,128)(2,1)S(1)} %get-tuple-element.53), channel_id=1, source_target_pairs={{0,128},{16,144},{32,160},{48,176},{64,192},{80,208},{96,224},{112... | collective-permute-start | bytes 6635528 | tf_op jit(solution)/shard_map/cond/branch_3_fun/ppermute | solution.py:23
Sparse Core Ops, SparseCore 0:
  10.4 57.2 all-gather.4
  70.1 51.7 all-gather.6
  129.4 88.2 reduce-scatter.4
  221.2 88.9 reduce-scatter.2
where the time goes:
time: 319 us; the launch traced here: 318 us
  waiting for transfers between devices  262 us (82%)
  matrix products  20.3 us (6%)
  between operations  14.5 us (5%)
  other arithmetic  13.8 us (4%)
  starting transfers between devices  5.14 us (2%)
    ppermute x3, waiting for transfers between devices, shifted(): lax.ppermute(x, axis, [(i, (i + by) % devices) for i in range(devices)])  140 us
    all_gather x1, waiting for transfers between devices, shards(): gathered = lax.all_gather(tokens_local, 'tp', axis=0, tiled=True)  59 us
    all_gather x1, waiting for transfers between devices, shards(): piece = lax.all_gather(grads_local, 'tp', axis=0, tiled=True)  48.9 us
    reduce_scatter x1, waiting for transfers between devices, shards(): lax.psum_scatter(jnp.dot(rows_hidden, down_w, preferred_element_type=jnp....  12.7 us
  transfers between devices with their start and end apart: 7, of which 6 were waited for; matrix products, arithmetic and copies ran while one was open for 8% of the time, Pallas kernels for 0%

commit v1 on v0

--- a/solution.py
+++ b/solution.py
@@ -37,7 +37,9 @@
     down_w = down_weight[0]
     width_scale = 1.0 / math.sqrt(D)
     hidden_scale = 1.0 / math.sqrt(FF)
-    gathered = lax.all_gather(tokens_local, "tp", axis=0, tiled=True)
+    gathered = jnp.concatenate(
+        lax.all_to_all(jnp.stack([tokens_local] * lax.axis_size("tp")), "tp", 0, 0), axis=0
+    )
     gate_pre = jnp.dot(gathered, gate_w, preferred_element_type=jnp.float32) * width_scale
     up_pre = jnp.dot(gathered, up_w, preferred_element_type=jnp.float32) * width_scale
     sigmoid_gate = jax.nn.sigmoid(gate_pre)

time: 319 us -> 282 us (0.88)
  waiting for transfers between devices: 262 us -> 213 us
  starting transfers between devices: 5.14 us -> 16.3 us
    all_gather x1 -> x0, waiting for transfers between devices: 59 us -> none  [shards(): gathered = lax.all_gather(tokens_local, 'tp', axis=0, tiled=True)]
    all_to_all x0 -> x1, waiting for transfers between devices: none -> 33.6 us  [shards(): lax.all_to_all(jnp.stack([tokens_local] * lax.axis_size('tp')), 'tp', 0, 0)]
    all_gather x1, waiting for transfers between devices: 48.9 us -> 26.7 us  [shards(): piece = lax.all_gather(grads_local, 'tp', axis=0, tiled=True)]
    all_to_all x0 -> x1, starting transfers between devices: none -> 11.2 us  [shards(): lax.all_to_all(jnp.stack([tokens_local] * lax.axis_size('tp')), 'tp', 0, 0)]
where the time goes in v1:
time: 282 us
  waiting for transfers between devices  213 us (76%)
  matrix products  19.1 us (7%)
  starting transfers between devices  16.3 us (6%)
  between operations  14.5 us (5%)
  other arithmetic  13.2 us (5%)
  local copies, waits for them, and re-layouts  5.24 us (2%)
    ppermute x3, waiting for transfers between devices, shifted(): lax.ppermute(x, axis, [(i, (i + by) % devices) for i in range(devices)])  140 us
    all_to_all x1, waiting for transfers between devices, shards(): lax.all_to_all(jnp.stack([tokens_local] * lax.axis_size('tp')), 'tp', 0, 0)  33.6 us
    all_gather x1, waiting for transfers between devices, shards(): piece = lax.all_gather(grads_local, 'tp', axis=0, tiled=True)  26.7 us
    reduce_scatter x1, waiting for transfers between devices, shards(): lax.psum_scatter(jnp.dot(rows_hidden, down_w, preferred_element_type=jnp....  12.5 us
    all_to_all x1, starting transfers between devices, shards(): lax.all_to_all(jnp.stack([tokens_local] * lax.axis_size('tp')), 'tp', 0, 0)  11.2 us
    broadcast_in_dim x1, other arithmetic, shards(): averaged[0][None]  5.69 us
  transfers between devices with their start and end apart: 7, of which 6 were waited for; matrix products, arithmetic and copies ran while one was open for 8% of the time, Pallas kernels for 0%

profile of v1, /device:TPU:6, one launch (start us, length us, event | category | flops | bytes accessed | tf_op | source)
XLA Modules:
  0.0 281.7 jit_solution(500434462123670620)
XLA Ops:
  7.2 0.0 copy-start.2
  7.2 2.2 stack.3
  9.4 11.2 %all-to-all-start = ((bf16[16,16,2560]{2,1,0:T(8,128)(2,1)}), bf16[16,16,2560]{2,1,0:T(8,128)(2,1)S(1)}, u32[]{:S(2)}, u32[]{:S(2)}) async-start(bf16[16,16,2560]{2,1,0:T(8,128)(2,1)} %stack.3), calls=%async_computation | async-start | bytes 2621440 | tf_op jit(solution)/shard_map/all_to_all | solution.py:41
  20.6 0.0 all-gather.3.cloned.1.call-start
  20.7 0.7 all-gather.3.cloned.1.call-update
  21.3 0.0 reduce-scatter.5.cloned.1.call-start
  21.4 33.6 %all-to-all-done = bf16[16,16,2560]{2,1,0:T(8,128)(2,1)S(1)} async-done(((bf16[16,16,2560]{2,1,0:T(8,128)(2,1)}), bf16[16,16,2560]{2,1,0:T(8,128)(2,1)S(1)}, u32[]{:S(2)}, u32[]{:S(2)}) %all-to-all-start) | async-done | bytes 1310752 | tf_op jit(solution)/shard_map/all_to_all | solution.py:41
  55.0 0.0 copy-start.3
  55.0 0.0 copy-done.2
  55.0 1.5 fusion.33
  56.6 0.1 copy-done.3
  56.6 1.5 fusion.30
  58.2 26.7 %all-gather.3.cloned.1.call-done = bf16[1,256,2560]{2,1,0:T(8,128)(2,1)} async-done(((bf16[1,16,2560]{2,1,0:T(8,128)(2,1)}), bf16[1,256,2560]{2,1,0:T(8,128)(2,1)}) %all-gather.3.cloned.1.call-update) | async-done | bytes 1310736 | tf_op jit(solution)/shard_map/all_gather | solution.py:55
  84.9 0.0 copy-start.4
  84.9 3.9 %multiply_convert_fusion = (bf16[256,432]{0,1:T(8,128)(2,1)S(1)}, bf16[256,432]{0,1:T(8,128)(2,1)S(1)}, bf16[256,432]{0,1:T(8,128)(2,1)}) fusion(f32[256,432]{0,1:T(8,128)} %fusion.30, f32[256,432]{0,1:T(8,128)} %fusion.33, bf16[1,432,2560]{2,1,0:T(8,128)(2,1)} %param.14, bf16[1,256,2560]{2,1,0:T(8,128)(2,1)} %all-gather.3.cloned.1.call-done), kind=kOutput, calls=%fused_computation.41 | convolution fusion | flops 568000512 | bytes 5070848 | tf_op jit(solution)/shard_map/td,fd->tf/dot_general | solution.py:58
  88.7 0.0 copy-start.9
  88.7 0.0 copy-start.11
  88.7 0.0 copy-done.4
  88.8 0.9 fusion.24
  89.6 0.0 copy-done.9
  89.6 0.0 copy-done.11
  89.6 2.4 fusion.14
  92.1 0.0 copy-start.6
  92.1 0.0 reduce-scatter.5.cloned.1.call-update
  92.1 0.0 reduce-scatter.3.cloned.1.call-start
  92.2 1.5 copy-done.6
  93.7 3.3 %convolution_multiply_fusion.3 = f32[256,2560]{1,0:T(8,128)} fusion(bf16[256,432]{0,1:T(8,128)(2,1)} %get-tuple-element.88, bf16[1,432,2560]{2,1,0:T(8,128)(2,1)S(1)} %copy-done.6), kind=kOutput, calls=%fused_computation.22 | convolution fusion | flops 566886400 | bytes 5054464 | tf_op jit(solution)/shard_map/dot_general | solution.py:50
  97.0 0.0 reduce-scatter.3.cloned.1.call-update
  97.7 0.0 copy-start.5
  97.7 0.0 copy-start.10
  97.7 2.6 fusion.11
  100.4 0.0 copy-done.5
  100.4 0.0 copy-done.10
  100.4 0.0 copy-start.7
  100.4 0.0 copy-start.8
  100.4 0.0 copy-start.12
  100.4 0.8 fusion.12
  101.2 0.9 copy-done.7
  102.1 0.0 copy-done.8
  102.1 0.5 copy-done.12
  102.5 0.0 copy-start
  102.5 2.1 fusion.13
  104.6 0.0 copy-done
  104.7 144.7 %conditional.4 = (bf16[2560,432]{0,1:T(8,128)(2,1)}, bf16[2560,432]{0,1:T(8,128)(2,1)}, bf16[432,2560]{1,0:T(8,128)(2,1)}) conditional(s32[]{:T(128)} %clamp.3, (bf16[2560,432]{0,1:T(8,128)(2,1)S(1)}, bf16[2560,432]{0,1:T(8,128)(2,1)S(1)}, bf16[432,2560]{1,0:T(8,128)(2,1)}) %tuple.58, ...), branch_computations={%region_2.3_spmd, %region_3.4_spmd, %region_4.5_spmd, %region_5.6_... | conditional | bytes 26542224
  104.7 1.4 collective-permute-start.9
  106.1 2.1 collective-permute-start.10
  108.2 1.4 collective-permute-start.11
  109.6 47.6 %collective-permute-done.9 = bf16[2560,432]{0,1:T(8,128)(2,1)} collective-permute-done((bf16[2560,432]{0,1:T(8,128)(2,1)S(1)}, bf16[2560,432]{0,1:T(8,128)(2,1)}, u32[]{:S(2)}, u32[]{:S(2)}) %collective-permute-start.9) | collective-permute-done | bytes 2211872 | tf_op jit(solution)/shard_map/cond/branch_3_fun/ppermute | solution.py:23
  157.2 47.4 %collective-permute-done.10 = bf16[2560,432]{0,1:T(8,128)(2,1)} collective-permute-done((bf16[2560,432]{0,1:T(8,128)(2,1)S(1)}, bf16[2560,432]{0,1:T(8,128)(2,1)}, u32[]{:S(2)}, u32[]{:S(2)}) %collective-permute-start.10) | collective-permute-done | bytes 2211872 | tf_op jit(solution)/shard_map/cond/branch_3_fun/ppermute | solution.py:23
  204.6 44.7 %collective-permute-done.11 = bf16[432,2560]{1,0:T(8,128)(2,1)} collective-permute-done((bf16[432,2560]{1,0:T(8,128)(2,1)}, bf16[432,2560]{1,0:T(8,128)(2,1)}, u32[]{:S(2)}, u32[]{:S(2)}) %collective-permute-start.11) | collective-permute-done | bytes 2211872 | tf_op jit(solution)/shard_map/cond/branch_3_fun/ppermute | solution.py:23
  249.3 0.0 copy-start.1
  249.3 4.4 %fusion.17 = bf16[1,432,2560]{2,1,0:T(8,128)(2,1)} fusion(bf16[432,2560]{1,0:T(8,128)(2,1)} %get-tuple-element.85, bf16[432,2560]{1,0:T(8,128)(2,1)} %fusion.13), kind=kLoop, calls=%fused_computation.25 | loop fusion | flops 5529600 | bytes 6635520 | tf_op jit(solution)/shard_map/broadcast_in_dim | solution.py:105
  253.8 0.0 copy-done.1
  253.8 5.7 %fusion.15 = (bf16[1,2560,432]{1,2,0:T(8,128)(2,1)}, bf16[1,2560,432]{1,2,0:T(8,128)(2,1)}) fusion(bf16[2560,432]{0,1:T(8,128)(2,1)} %get-tuple-element.83, bf16[2560,432]{0,1:T(8,128)(2,1)S(1)} %copy-done.1, bf16[2560,432]{0,1:T(8,128)(2,1)} %get-tuple-element.84, bf16[2560,432]{0,1:T(8,128)(2,1)S(1)} %fusion.11), kind=kLoop, calls=%fused_computation.23 | loop fusion | flops 11059200 | bytes 13271040 | tf_op jit(solution)/shard_map/broadcast_in_dim | solution.py:103
  259.5 0.0 reduce-scatter.5.cloned.1.call-done
  259.5 1.6 convert_bitcast_fusion
  261.0 12.5 %reduce-scatter.3.cloned.1.call-done = f32[16,2560]{1,0:T(8,128)} async-done(((f32[256,2560]{1,0:T(8,128)}), f32[16,2560]{1,0:T(8,128)}) %reduce-scatter.3.cloned.1.call-update) | async-done | bytes 163856 | tf_op jit(solution)/shard_map/reduce_scatter | solution.py:49
  273.6 1.6 convert_bitcast_fusion.1
Async XLA Ops:
  7.2 47.9 %copy-start.2 = (bf16[1,2560,432]{1,2,0:T(8,128)(2,1)S(1)}, bf16[1,2560,432]{1,2,0:T(8,128)(2,1)}, u32[]{:S(2)}) copy-start(bf16[1,2560,432]{1,2,0:T(8,128)(2,1)} %param.13) | copy-start | bytes 6635524
  9.4 45.6 %all-to-all-start = ((bf16[16,16,2560]{2,1,0:T(8,128)(2,1)}), bf16[16,16,2560]{2,1,0:T(8,128)(2,1)S(1)}, u32[]{:S(2)}, u32[]{:S(2)}) async-start(bf16[16,16,2560]{2,1,0:T(8,128)(2,1)} %stack.3), calls=%async_computation | async-start | bytes 2621440 | tf_op jit(solution)/shard_map/all_to_all | solution.py:41
  20.6 64.3 %all-gather.3.cloned.1.call-start = ((), (), s32[]{:S(2)}) async-start(), calls=%async_computation.5 | async-start | bytes 1392640 | tf_op jit(solution)/shard_map/all_gather | solution.py:55
  21.3 238.1 %reduce-scatter.5.cloned.1.call-start = ((), (), s32[]{:S(2)}) async-start(), calls=%async_computation.4 | async-start | bytes 2785280 | tf_op jit(solution)/shard_map/reduce_scatter | solution.py:72
  55.0 1.6 copy-start.3
  84.9 3.9 %copy-start.4 = (bf16[1,2560,432]{1,2,0:T(8,128)(2,1)S(1)}, bf16[1,2560,432]{1,2,0:T(8,128)(2,1)}, u32[]{:S(2)}) copy-start(bf16[1,2560,432]{1,2,0:T(8,128)(2,1)} %param.12) | copy-start | bytes 6635524
  88.7 0.9 copy-start.9
  88.7 0.9 copy-start.11
  92.1 1.6 copy-start.6
  92.1 181.5 %reduce-scatter.3.cloned.1.call-start = ((), (), s32[]{:S(2)}) async-start(), calls=%async_computation.3 | async-start | bytes 2785280 | tf_op jit(solution)/shard_map/reduce_scatter | solution.py:49
  97.7 2.7 copy-start.5
  97.7 2.7 copy-start.10
  100.4 1.7 copy-start.7
  100.4 1.7 copy-start.8
  100.4 2.1 copy-start.12
  102.5 2.1 copy-start
  104.7 52.6 %collective-permute-start.9 = (bf16[2560,432]{0,1:T(8,128)(2,1)S(1)}, bf16[2560,432]{0,1:T(8,128)(2,1)}, u32[]{:S(2)}, u32[]{:S(2)}) collective-permute-start(bf16[2560,432]{0,1:T(8,128)(2,1)S(1)} %get-tuple-element.51), channel_id=1, source_target_pairs={{0,128},{16,144},{32,160},{48,176},{64,192},{80,208},{96,224},{112... | collective-permute-start | bytes 6635528 | tf_op jit(solution)/shard_map/cond/branch_3_fun/ppermute | solution.py:23
  106.1 98.5 %collective-permute-start.10 = (bf16[2560,432]{0,1:T(8,128)(2,1)S(1)}, bf16[2560,432]{0,1:T(8,128)(2,1)}, u32[]{:S(2)}, u32[]{:S(2)}) collective-permute-start(bf16[2560,432]{0,1:T(8,128)(2,1)S(1)} %get-tuple-element.52), channel_id=1, source_target_pairs={{0,128},{16,144},{32,160},{48,176},{64,192},{80,208},{96,224},{112... | collective-permute-start | bytes 6635528 | tf_op jit(solution)/shard_map/cond/branch_3_fun/ppermute | solution.py:23
  108.2 141.2 %collective-permute-start.11 = (bf16[432,2560]{1,0:T(8,128)(2,1)}, bf16[432,2560]{1,0:T(8,128)(2,1)}, u32[]{:S(2)}, u32[]{:S(2)}) collective-permute-start(bf16[432,2560]{1,0:T(8,128)(2,1)} %get-tuple-element.53), channel_id=1, source_target_pairs={{0,128},{16,144},{32,160},{48,176},{64,192},{80,208},{96,224},{112... | collective-permute-start | bytes 6635528 | tf_op jit(solution)/shard_map/cond/branch_3_fun/ppermute | solution.py:23
  249.3 4.4 %copy-start.1 = (bf16[2560,432]{0,1:T(8,128)(2,1)S(1)}, bf16[2560,432]{0,1:T(8,128)(2,1)}, u32[]{:S(2)}) copy-start(bf16[2560,432]{0,1:T(8,128)(2,1)} %copy-done) | copy-start | bytes 6635524
Sparse Core Ops, SparseCore 0:
  23.8 60.9 all-gather.2
  92.2 88.7 reduce-scatter.4
  184.6 88.9 reduce-scatter.2
